TPU v7x, 32 devices: a whole 2x2x4 slice. The times are simulated.
32 devices in a mesh: section: 4 (over z), head: 8 (over y, x, core).
Axes of the slice: x: 2, y: 2, z: 4, core: 2. Of those that a mesh axis runs over, the one named last changes fastest.
Arguments:
- prompt_states: bfloat16 [1, 128, 8192], P(None, 'head'), may hold values from -6 to 6
- norm_gain: float32 [4, 8192], P('section'), may hold values from 0.1 to 1.9
- query_weight: bfloat16 [4, 8192, 8192], P('section', None, 'head')
- key_weight: bfloat16 [4, 8192, 1024], P('section', None, 'head')
- value_weight: bfloat16 [4, 8192, 1024], P('section', None, 'head'), may hold values from -0.0625 to 0.0625
- out_weight: bfloat16 [4, 8192, 8192], P('section', 'head'), may hold values from -1 to 1
- cache_keys: bfloat16 [4, 4096, 1024], P('section', None, 'head'), may hold values from -6 to 6
- cache_values: bfloat16 [4, 4096, 1024], P('section', None, 'head'), may hold values from -6 to 6
- block_lists: int32 [1, 8], replicated, may hold values from 0 to 32, as said below
Outputs:
- section_states: bfloat16 [4, 1, 128, 8192], P('section', None, 'head')
Inputs may be any that keep to these rules, and one draw needn't show every extreme that they name: `block_lists`: row i lists 8 distinct key blocks; block 32 + i is among them and none is greater.
All inputs are finite; a program needn't handle non-finite values.
Results may differ from a plain program's by a relative error of at most 0.024.
Values may be sent and summed in bfloat16 or wider, within the bound.
No kernel may reach another device: no remote copies, remote signals or barrier semaphores. Data moves between devices by JAX's collectives and lax.ppermute only.
A program may use at most 128 MiB of HBM per device.

v0:
```python
import math

import jax
import jax.numpy as jnp
from jax import lax
from jax.sharding import PartitionSpec as P

HD = 128
BLOCK = 128
SPAN = 128
PREFIX = 4096


EPS = 1e-05
THETA = 500000.0


def shortened(array):

    def short(part):
        return part.astype(jnp.bfloat16) if part.dtype == jnp.float32 else part

    return jax.tree.map(short, array)


def swapped(block, axis, distance):
    count = lax.axis_size(axis)
    route = []
    for low in range(count):
        high = low | 1 << distance
        if high != low and high < count:
            route += [(low, high), (high, low)]
    return lax.ppermute(block, axis, route)


def from_behind(value, axis, steps):
    count = lax.axis_size(axis)
    first, last = (max(0, -steps), min(count, count - steps))
    return lax.ppermute(value, axis, [(source, source + steps) for source in range(first, last)])


def rotary(values, cosine, sine_rows):
    half_dim = values.shape[-1] // 2
    first_half = values[..., :half_dim]
    second_half = values[..., half_dim:]
    return jnp.concatenate(
        [
            first_half * cosine - second_half * sine_rows,
            second_half * cosine + first_half * sine_rows,
        ],
        -1,
    )


def pair_up(own_part, partner, bit_number, head_index):
    is_lower = head_index >> bit_number & 1 == 0
    return jnp.where(
        is_lower, jnp.concatenate([own_part, partner], -1), jnp.concatenate([partner, own_part], -1)
    )


def join_cache(key_part, value_part, group_bits, head_index):
    for bit_number in range(group_bits):
        other_keys, other_values = (
            swapped(shortened(key_part), "head", bit_number).astype(key_part.dtype),
            swapped(shortened(value_part), "head", bit_number).astype(value_part.dtype),
        )
        key_part = pair_up(key_part, other_keys, bit_number, head_index)
        value_part = pair_up(value_part, other_values, bit_number, head_index)
    return (key_part, value_part)


def join_weights(key_part, value_part, group_bits, head_index):
    for bit_number in range(group_bits):
        other_keys, other_values = (
            swapped(shortened(key_part), "head", bit_number).astype(key_part.dtype),
            swapped(shortened(value_part), "head", bit_number).astype(value_part.dtype),
        )
        key_part = pair_up(key_part, other_keys, bit_number, head_index)
        value_part = pair_up(value_part, other_values, bit_number, head_index)
    return (key_part, value_part)


def on_device(
    prompt_states,
    norm_gain,
    query_weight,
    key_weight,
    value_weight,
    out_weight,
    cache_keys,
    cache_values,
    block_lists,
):
    sections = lax.axis_size("section")
    section_index = lax.axis_index("section")
    head_index = lax.axis_index("head")
    span_count = prompt_states.shape[0]
    local_rows = prompt_states.shape[1]
    width = prompt_states.shape[2]
    kv_cols = key_weight.shape[2]
    group_bits = (HD // kv_cols).bit_length() - 1
    query_cols = query_weight.shape[2]
    query_heads = query_cols // HD
    gain_row = norm_gain[0]
    query_matrix = query_weight[0]
    out_matrix = out_weight[0]
    scale = 1.0 / math.sqrt(HD)
    blocks_per_span = SPAN // BLOCK
    keys_prefix, values_prefix = join_cache(cache_keys[0], cache_values[0], group_bits, head_index)
    key_matrix, value_matrix = join_weights(key_weight[0], value_weight[0], group_bits, head_index)
    key_cols = key_matrix.shape[1]
    window_zeros = jnp.zeros((span_count * SPAN, HD), jnp.bfloat16)
    key_store = jnp.concatenate([keys_prefix, window_zeros], 0)
    value_store = jnp.concatenate([values_prefix, window_zeros], 0)
    inverse_freq = jnp.exp(-math.log(THETA) * jnp.arange(HD // 2, dtype=jnp.float32) * 2.0 / HD)
    send_rows = jnp.zeros((local_rows, width), jnp.bfloat16)
    outputs = jnp.zeros((span_count, local_rows, width), jnp.bfloat16)

    def project(rows_piece):
        return jnp.concatenate(
            [
                jnp.dot(rows_piece, query_matrix, preferred_element_type=jnp.float32),
                jnp.dot(rows_piece, key_matrix, preferred_element_type=jnp.float32),
                jnp.dot(rows_piece, value_matrix, preferred_element_type=jnp.float32),
            ],
            1,
        )

    def step(step_number, loop_state):
        send_rows, key_store, value_store, outputs = loop_state
        span_step = step_number - section_index
        is_valid = (span_step >= 0) & (span_step < span_count)
        current = jnp.clip(span_step, 0, span_count - 1)
        incoming = from_behind(send_rows, "section", 1)
        fresh_rows = lax.dynamic_index_in_dim(prompt_states, current, 0, keepdims=False)
        states = jnp.where(section_index == 0, fresh_rows, incoming)
        widened = states.astype(jnp.float32)
        normed = (
            widened * lax.rsqrt(jnp.mean(widened * widened, -1, keepdims=True) + EPS) * gain_row
        ).astype(jnp.bfloat16)
        projected = project(lax.all_gather(normed, "head", axis=0, tiled=True))
        queries = projected[:, :query_cols]
        key_raw = projected[:, query_cols : query_cols + key_cols].astype(jnp.bfloat16)
        new_values = projected[:, query_cols + key_cols :].astype(jnp.bfloat16)
        key_raw = lax.optimization_barrier(key_raw)
        first_row = PREFIX + current * SPAN
        positions = first_row + jnp.arange(SPAN, dtype=jnp.int32)
        angles = positions.astype(jnp.float32)[:, None] * inverse_freq[None, :]
        cosine = jnp.cos(angles)[:, None, :]
        sine_rows = jnp.sin(angles)[:, None, :]
        queries = rotary(queries.reshape(SPAN, query_heads, HD), cosine, sine_rows).astype(
            jnp.bfloat16
        )
        new_keys = rotary(key_raw.astype(jnp.float32)[:, None, :], cosine, sine_rows)[:, 0].astype(
            jnp.bfloat16
        )
        old_keys = lax.dynamic_slice_in_dim(key_store, first_row, SPAN, 0)
        key_store = lax.dynamic_update_slice_in_dim(
            key_store, jnp.where(is_valid, new_keys, old_keys), first_row, 0
        )
        old_values = lax.dynamic_slice_in_dim(value_store, first_row, SPAN, 0)
        value_store = lax.dynamic_update_slice_in_dim(
            value_store, jnp.where(is_valid, new_values, old_values), first_row, 0
        )
        key_blocks = key_store.reshape(-1, BLOCK, HD)[block_lists].reshape(blocks_per_span, -1, HD)
        value_blocks = value_store.reshape(-1, BLOCK, HD)[block_lists].reshape(
            blocks_per_span, -1, HD
        )
        key_positions = (
            block_lists[:, :, None] * BLOCK + jnp.arange(BLOCK, dtype=jnp.int32)[None, None, :]
        ).reshape(blocks_per_span, -1)
        query_positions = positions.reshape(blocks_per_span, BLOCK)
        grouped = queries.reshape(blocks_per_span, BLOCK, query_heads, HD)
        scores = (
            jnp.einsum("abhd,and->ahbn", grouped, key_blocks, preferred_element_type=jnp.float32)
            * scale
        )
        allowed = key_positions[:, None, None, :] <= query_positions[:, None, :, None]
        scores = jnp.where(allowed, scores, -1e30)
        row_peak = jnp.max(scores, -1, keepdims=True)
        probabilities = jnp.exp(scores - row_peak)
        totals = jnp.sum(probabilities, -1)
        weights = probabilities.astype(jnp.bfloat16)
        mixed = jnp.einsum(
            "ahbn,and->abhd", weights, value_blocks, preferred_element_type=jnp.float32
        )
        mixed = mixed / jnp.transpose(totals, (0, 2, 1))[..., None]
        attended = mixed.reshape(SPAN, query_cols).astype(jnp.bfloat16)
        summed = lax.psum_scatter(
            jnp.dot(attended, out_matrix, preferred_element_type=jnp.float32).astype(jnp.bfloat16),
            "head",
            scatter_dimension=0,
            tiled=True,
        ).astype(jnp.float32)
        updated = (widened + summed).astype(jnp.bfloat16)
        old_out = lax.dynamic_index_in_dim(outputs, current, 0, keepdims=False)
        outputs = lax.dynamic_update_index_in_dim(
            outputs, jnp.where(is_valid, updated, old_out), current, 0
        )
        return (updated, key_store, value_store, outputs)

    final_state = lax.fori_loop(
        0, span_count + sections - 1, step, (send_rows, key_store, value_store, outputs)
    )
    return final_state[3][None]


def solution(mesh):
    return jax.shard_map(
        on_device,
        mesh=mesh,
        in_specs=(
            P(None, "head", None),
            P("section", None),
            P("section", None, "head"),
            P("section", None, "head"),
            P("section", None, "head"),
            P("section", "head", None),
            P("section", None, "head"),
            P("section", None, "head"),
            P(),
        ),
        out_specs=P("section", None, "head", None),
        check_vma=False,
    )
```

profile of v0, /device:TPU:25, one launch (start us, length us, event | category | flops | bytes accessed | tf_op | source)
XLA Modules:
  0.0 504.4 jit_solution(4211756073315949870)
XLA Ops:
  6.5 1.6 copy.34
  10.6 487.0 %while.23 = (s32[]{:T(128)}, bf16[16,8192]{1,0:T(8,128)(2,1)}, bf16[4224,128]{0,1:T(8,128)(2,1)S(1)}, bf16[4224,128]{0,1:T(8,128)(2,1)}, bf16[1,16,8192]{2,1,0:T...) while((s32[]{:T(128)}, bf16[16,8192]{1,0:T(8,128)(2,1)}, ...), condition=%wide.region_5.6_spmd.clone.clone, body=%wide.region_0.5_spmd.clone.clone.sunk | while | flops 5384798720 | bytes 122106280 | solution.py:203
  10.6 1.3 collective-permute-start
  11.9 7.8 %collective-permute-done = bf16[16,8192]{1,0:T(8,128)(2,1)S(1)} collective-permute-done((bf16[16,8192]{1,0:T(8,128)(2,1)S(1)}, bf16[16,8192]{1,0:T(8,128)(2,1)S(1)}, u32[]{:S(2)}, u32[]{:S(2)}) %collective-permute-start) | collective-permute-done | bytes 262176 | tf_op jit(solution)/shard_map/while/body/eval_jaxpr/ppermute | solution.py:39
  20.8 1.6 fusion.88
  22.5 2.4 copy.59
  27.8 25.0 %all-gather.2.cloned.1.call-done = bf16[128,8192]{1,0:T(8,128)(2,1)} async-done(((bf16[16,8192]{1,0:T(8,128)(2,1)}), bf16[128,8192]{1,0:T(8,128)(2,1)}) %all-gather.2.cloned.1.call-update) | async-done | bytes 2097168 | tf_op jit(solution)/shard_map/while/body/eval_jaxpr/all_gather | solution.py:142
  52.8 3.3 convolution_convert_fusion.5
  57.8 8.2 %convolution_bitcast_fusion.2 = f32[16,8,8,128]{3,1,2,0:T(8,128)S(1)} fusion(bf16[128,8192]{1,0:T(8,128)(2,1)S(1)} %copy-done, bf16[8192,1024]{1,0:T(8,128)(2,1)} %get-tuple-element.651), kind=kOutput, calls=%fused_computation.13.clone.1 | convolution fusion | flops 2147483648 | bytes 19398656 | tf_op jit(solution)/shard_map/while/body/eval_jaxpr/dot_general | solution.py:123
  66.9 1.7 fusion.89
  69.4 1.4 fusion.93
  72.9 1.3 gather_fusion.1
  75.3 1.8 fusion.94
  79.2 9.6 %convolution_convert_fusion.6 = bf16[128,8192]{1,0:T(8,128)(2,1)} fusion(bf16[128,1024]{0,1:T(8,128)(2,1)S(1)} %bitcast.170, bf16[1024,8192]{1,0:T(8,128)(2,1)} %get-tuple-element.652), kind=kOutput, calls=%fused_computation.3.clone.1 | convolution fusion | flops 2148532224 | bytes 19136512 | tf_op jit(solution)/shard_map/while/body/eval_jaxpr/dot_general | solution.py:191
  88.8 1.6 copy.65
  91.4 38.3 %reduce-scatter.2.cloned.1.call-done = bf16[16,8192]{1,0:T(8,128)(2,1)} async-done(((bf16[128,8192]{1,0:T(8,128)(2,1)}), bf16[16,8192]{1,0:T(8,128)(2,1)}) %reduce-scatter.2.cloned.1.call-update) | async-done | bytes 262160 | tf_op jit(solution)/shard_map/while/body/eval_jaxpr/reduce_scatter | solution.py:190
  129.7 1.8 fusion.97
  133.4 1.3 collective-permute-start
  134.7 7.7 %collective-permute-done = bf16[16,8192]{1,0:T(8,128)(2,1)S(1)} collective-permute-done((bf16[16,8192]{1,0:T(8,128)(2,1)S(1)}, bf16[16,8192]{1,0:T(8,128)(2,1)S(1)}, u32[]{:S(2)}, u32[]{:S(2)}) %collective-permute-start) | collective-permute-done | bytes 262176 | tf_op jit(solution)/shard_map/while/body/eval_jaxpr/ppermute | solution.py:39
  143.6 1.6 fusion.88
  145.3 2.4 copy.59
  150.5 24.0 %all-gather.2.cloned.1.call-done = bf16[128,8192]{1,0:T(8,128)(2,1)} async-done(((bf16[16,8192]{1,0:T(8,128)(2,1)}), bf16[128,8192]{1,0:T(8,128)(2,1)}) %all-gather.2.cloned.1.call-update) | async-done | bytes 2097168 | tf_op jit(solution)/shard_map/while/body/eval_jaxpr/all_gather | solution.py:142
  174.6 3.3 convolution_convert_fusion.5
  179.6 8.2 %convolution_bitcast_fusion.2 = f32[16,8,8,128]{3,1,2,0:T(8,128)S(1)} fusion(bf16[128,8192]{1,0:T(8,128)(2,1)S(1)} %copy-done, bf16[8192,1024]{1,0:T(8,128)(2,1)} %get-tuple-element.651), kind=kOutput, calls=%fused_computation.13.clone.1 | convolution fusion | flops 2147483648 | bytes 19398656 | tf_op jit(solution)/shard_map/while/body/eval_jaxpr/dot_general | solution.py:123
  188.7 1.7 fusion.89
  191.2 1.4 fusion.93
  192.7 1.3 gather_fusion
  194.7 1.3 gather_fusion.1
  197.0 1.8 fusion.94
  201.0 9.6 %convolution_convert_fusion.6 = bf16[128,8192]{1,0:T(8,128)(2,1)} fusion(bf16[128,1024]{0,1:T(8,128)(2,1)S(1)} %bitcast.170, bf16[1024,8192]{1,0:T(8,128)(2,1)} %get-tuple-element.652), kind=kOutput, calls=%fused_computation.3.clone.1 | convolution fusion | flops 2148532224 | bytes 19136512 | tf_op jit(solution)/shard_map/while/body/eval_jaxpr/dot_general | solution.py:191
  210.6 1.6 copy.65
  213.2 38.3 %reduce-scatter.2.cloned.1.call-done = bf16[16,8192]{1,0:T(8,128)(2,1)} async-done(((bf16[128,8192]{1,0:T(8,128)(2,1)}), bf16[16,8192]{1,0:T(8,128)(2,1)}) %reduce-scatter.2.cloned.1.call-update) | async-done | bytes 262160 | tf_op jit(solution)/shard_map/while/body/eval_jaxpr/reduce_scatter | solution.py:190
  251.5 1.8 fusion.97
  255.1 1.3 collective-permute-start
  256.4 7.7 %collective-permute-done = bf16[16,8192]{1,0:T(8,128)(2,1)S(1)} collective-permute-done((bf16[16,8192]{1,0:T(8,128)(2,1)S(1)}, bf16[16,8192]{1,0:T(8,128)(2,1)S(1)}, u32[]{:S(2)}, u32[]{:S(2)}) %collective-permute-start) | collective-permute-done | bytes 262176 | tf_op jit(solution)/shard_map/while/body/eval_jaxpr/ppermute | solution.py:39
  265.3 1.6 fusion.88
  267.0 2.4 copy.59
  272.3 24.1 %all-gather.2.cloned.1.call-done = bf16[128,8192]{1,0:T(8,128)(2,1)} async-done(((bf16[16,8192]{1,0:T(8,128)(2,1)}), bf16[128,8192]{1,0:T(8,128)(2,1)}) %all-gather.2.cloned.1.call-update) | async-done | bytes 2097168 | tf_op jit(solution)/shard_map/while/body/eval_jaxpr/all_gather | solution.py:142
  296.3 3.3 convolution_convert_fusion.5
  301.4 8.2 %convolution_bitcast_fusion.2 = f32[16,8,8,128]{3,1,2,0:T(8,128)S(1)} fusion(bf16[128,8192]{1,0:T(8,128)(2,1)S(1)} %copy-done, bf16[8192,1024]{1,0:T(8,128)(2,1)} %get-tuple-element.651), kind=kOutput, calls=%fused_computation.13.clone.1 | convolution fusion | flops 2147483648 | bytes 19398656 | tf_op jit(solution)/shard_map/while/body/eval_jaxpr/dot_general | solution.py:123
  310.5 1.7 fusion.89
  313.0 1.4 fusion.93
  316.5 1.3 gather_fusion.1
  318.8 1.8 fusion.94
  322.7 9.6 %convolution_convert_fusion.6 = bf16[128,8192]{1,0:T(8,128)(2,1)} fusion(bf16[128,1024]{0,1:T(8,128)(2,1)S(1)} %bitcast.170, bf16[1024,8192]{1,0:T(8,128)(2,1)} %get-tuple-element.652), kind=kOutput, calls=%fused_computation.3.clone.1 | convolution fusion | flops 2148532224 | bytes 19136512 | tf_op jit(solution)/shard_map/while/body/eval_jaxpr/dot_general | solution.py:191
  332.4 1.6 copy.65
  335.0 38.3 %reduce-scatter.2.cloned.1.call-done = bf16[16,8192]{1,0:T(8,128)(2,1)} async-done(((bf16[128,8192]{1,0:T(8,128)(2,1)}), bf16[16,8192]{1,0:T(8,128)(2,1)}) %reduce-scatter.2.cloned.1.call-update) | async-done | bytes 262160 | tf_op jit(solution)/shard_map/while/body/eval_jaxpr/reduce_scatter | solution.py:190
  373.3 1.8 fusion.97
  376.9 1.3 collective-permute-start
  378.2 7.7 %collective-permute-done = bf16[16,8192]{1,0:T(8,128)(2,1)S(1)} collective-permute-done((bf16[16,8192]{1,0:T(8,128)(2,1)S(1)}, bf16[16,8192]{1,0:T(8,128)(2,1)S(1)}, u32[]{:S(2)}, u32[]{:S(2)}) %collective-permute-start) | collective-permute-done | bytes 262176 | tf_op jit(solution)/shard_map/while/body/eval_jaxpr/ppermute | solution.py:39
  387.1 1.6 fusion.88
  388.8 2.4 copy.59
  394.1 24.0 %all-gather.2.cloned.1.call-done = bf16[128,8192]{1,0:T(8,128)(2,1)} async-done(((bf16[16,8192]{1,0:T(8,128)(2,1)}), bf16[128,8192]{1,0:T(8,128)(2,1)}) %all-gather.2.cloned.1.call-update) | async-done | bytes 2097168 | tf_op jit(solution)/shard_map/while/body/eval_jaxpr/all_gather | solution.py:142
  418.1 3.3 convolution_convert_fusion.5
  423.1 8.2 %convolution_bitcast_fusion.2 = f32[16,8,8,128]{3,1,2,0:T(8,128)S(1)} fusion(bf16[128,8192]{1,0:T(8,128)(2,1)S(1)} %copy-done, bf16[8192,1024]{1,0:T(8,128)(2,1)} %get-tuple-element.651), kind=kOutput, calls=%fused_computation.13.clone.1 | convolution fusion | flops 2147483648 | bytes 19398656 | tf_op jit(solution)/shard_map/while/body/eval_jaxpr/dot_general | solution.py:123
  432.3 1.7 fusion.89
  434.8 1.4 fusion.93
  436.2 1.3 gather_fusion
  438.2 1.3 gather_fusion.1
  440.6 1.8 fusion.94
  444.5 9.6 %convolution_convert_fusion.6 = bf16[128,8192]{1,0:T(8,128)(2,1)} fusion(bf16[128,1024]{0,1:T(8,128)(2,1)S(1)} %bitcast.170, bf16[1024,8192]{1,0:T(8,128)(2,1)} %get-tuple-element.652), kind=kOutput, calls=%fused_computation.3.clone.1 | convolution fusion | flops 2148532224 | bytes 19136512 | tf_op jit(solution)/shard_map/while/body/eval_jaxpr/dot_general | solution.py:191
  454.1 1.6 copy.65
  456.7 38.3 %reduce-scatter.2.cloned.1.call-done = bf16[16,8192]{1,0:T(8,128)(2,1)} async-done(((bf16[128,8192]{1,0:T(8,128)(2,1)}), bf16[16,8192]{1,0:T(8,128)(2,1)}) %reduce-scatter.2.cloned.1.call-update) | async-done | bytes 262160 | tf_op jit(solution)/shard_map/while/body/eval_jaxpr/reduce_scatter | solution.py:190
  495.1 1.8 fusion.97
  (199 shorter events, 60.1 us)
Async XLA Ops:
  6.5 1.7 copy-start.9
  8.2 2.3 copy-start.10
  10.6 14.3 %copy-start.3 = (bf16[4224,128]{0,1:T(8,128)(2,1)}, bf16[4224,128]{0,1:T(8,128)(2,1)S(1)}, u32[]{:S(2)}) copy-start(bf16[4224,128]{0,1:T(8,128)(2,1)S(1)} %get-tuple-element.622) | copy-start | bytes 3244036 | tf_op jit(solution)/shard_map/while
  10.6 42.2 %all-gather.2.cloned.1.call-start = ((), (), s32[]{:S(2)}) async-start(), calls=%async_computation.1 | async-start | bytes 2359296 | tf_op jit(solution)/shard_map/while/body/eval_jaxpr/all_gather | solution.py:142
  10.6 9.1 %collective-permute-start = (bf16[16,8192]{1,0:T(8,128)(2,1)S(1)}, bf16[16,8192]{1,0:T(8,128)(2,1)S(1)}, u32[]{:S(2)}, u32[]{:S(2)}) collective-permute-start(bf16[16,8192]{1,0:T(8,128)(2,1)S(1)} %broadcast_select_fusion.2), channel_id=1, source_target_pairs={{0,8},{8,16},{16,24},{1,9},{9,17},{17,25},{2,10},{10,18},{18,26},{... | collective-permute-start | bytes 786440 | tf_op jit(solution)/shard_map/while/body/eval_jaxpr/ppermute | solution.py:39
  22.4 107.3 %reduce-scatter.2.cloned.1.call-start = ((), (), s32[]{:S(2)}) async-start(), calls=%async_computation.2 | async-start | bytes 2359296 | tf_op jit(solution)/shard_map/while/body/eval_jaxpr/reduce_scatter | solution.py:190
  52.8 5.0 copy-start
  57.8 9.1 %copy-start.2 = (bf16[8192,128]{1,0:T(8,128)(2,1)S(1)}, bf16[8192,128]{1,0:T(8,128)(2,1)}, u32[]{:S(2)}) copy-start(bf16[8192,128]{1,0:T(8,128)(2,1)} %get-tuple-element.648) | copy-start | bytes 6291460 | tf_op jit(solution)/shard_map/while
  68.7 2.1 copy-start.1
  69.4 1.4 copy-start.8
  75.2 1.9 copy-start.4
  77.1 1.0 copy-start.7
  88.8 40.9 %copy-start.5 = (bf16[1,16,8192]{2,1,0:T(8,128)(2,1)S(1)}, bf16[1,16,8192]{2,1,0:T(8,128)(2,1)}, u32[]{:S(2)}) copy-start(bf16[1,16,8192]{2,1,0:T(8,128)(2,1)} %get-tuple-element.624) | copy-start | bytes 786436 | tf_op jit(solution)/shard_map/while
  131.5 0.7 copy-start.6
  132.2 15.4 %copy-start.3 = (bf16[4224,128]{0,1:T(8,128)(2,1)}, bf16[4224,128]{0,1:T(8,128)(2,1)S(1)}, u32[]{:S(2)}) copy-start(bf16[4224,128]{0,1:T(8,128)(2,1)S(1)} %get-tuple-element.622) | copy-start | bytes 3244036 | tf_op jit(solution)/shard_map/while
  132.2 42.3 %all-gather.2.cloned.1.call-start = ((), (), s32[]{:S(2)}) async-start(), calls=%async_computation.1 | async-start | bytes 2359296 | tf_op jit(solution)/shard_map/while/body/eval_jaxpr/all_gather | solution.py:142
  133.4 9.0 %collective-permute-start = (bf16[16,8192]{1,0:T(8,128)(2,1)S(1)}, bf16[16,8192]{1,0:T(8,128)(2,1)S(1)}, u32[]{:S(2)}, u32[]{:S(2)}) collective-permute-start(bf16[16,8192]{1,0:T(8,128)(2,1)S(1)} %broadcast_select_fusion.2), channel_id=1, source_target_pairs={{0,8},{8,16},{16,24},{1,9},{9,17},{17,25},{2,10},{10,18},{18,26},{... | collective-permute-start | bytes 786440 | tf_op jit(solution)/shard_map/while/body/eval_jaxpr/ppermute | solution.py:39
  145.2 106.3 %reduce-scatter.2.cloned.1.call-start = ((), (), s32[]{:S(2)}) async-start(), calls=%async_computation.2 | async-start | bytes 2359296 | tf_op jit(solution)/shard_map/while/body/eval_jaxpr/reduce_scatter | solution.py:190
  174.6 5.0 copy-start
  179.6 9.1 %copy-start.2 = (bf16[8192,128]{1,0:T(8,128)(2,1)S(1)}, bf16[8192,128]{1,0:T(8,128)(2,1)}, u32[]{:S(2)}) copy-start(bf16[8192,128]{1,0:T(8,128)(2,1)} %get-tuple-element.648) | copy-start | bytes 6291460 | tf_op jit(solution)/shard_map/while
  190.5 2.1 copy-start.1
  191.2 1.4 copy-start.8
  197.0 1.9 copy-start.4
  198.9 1.0 copy-start.7
  210.6 40.9 %copy-start.5 = (bf16[1,16,8192]{2,1,0:T(8,128)(2,1)S(1)}, bf16[1,16,8192]{2,1,0:T(8,128)(2,1)}, u32[]{:S(2)}) copy-start(bf16[1,16,8192]{2,1,0:T(8,128)(2,1)} %get-tuple-element.624) | copy-start | bytes 786436 | tf_op jit(solution)/shard_map/while
  253.3 0.7 copy-start.6
  254.0 15.4 %copy-start.3 = (bf16[4224,128]{0,1:T(8,128)(2,1)}, bf16[4224,128]{0,1:T(8,128)(2,1)S(1)}, u32[]{:S(2)}) copy-start(bf16[4224,128]{0,1:T(8,128)(2,1)S(1)} %get-tuple-element.622) | copy-start | bytes 3244036 | tf_op jit(solution)/shard_map/while
  254.0 42.4 %all-gather.2.cloned.1.call-start = ((), (), s32[]{:S(2)}) async-start(), calls=%async_computation.1 | async-start | bytes 2359296 | tf_op jit(solution)/shard_map/while/body/eval_jaxpr/all_gather | solution.py:142
  255.1 9.0 %collective-permute-start = (bf16[16,8192]{1,0:T(8,128)(2,1)S(1)}, bf16[16,8192]{1,0:T(8,128)(2,1)S(1)}, u32[]{:S(2)}, u32[]{:S(2)}) collective-permute-start(bf16[16,8192]{1,0:T(8,128)(2,1)S(1)} %broadcast_select_fusion.2), channel_id=1, source_target_pairs={{0,8},{8,16},{16,24},{1,9},{9,17},{17,25},{2,10},{10,18},{18,26},{... | collective-permute-start | bytes 786440 | tf_op jit(solution)/shard_map/while/body/eval_jaxpr/ppermute | solution.py:39
  267.0 106.3 %reduce-scatter.2.cloned.1.call-start = ((), (), s32[]{:S(2)}) async-start(), calls=%async_computation.2 | async-start | bytes 2359296 | tf_op jit(solution)/shard_map/while/body/eval_jaxpr/reduce_scatter | solution.py:190
  296.3 5.0 copy-start
  301.4 9.1 %copy-start.2 = (bf16[8192,128]{1,0:T(8,128)(2,1)S(1)}, bf16[8192,128]{1,0:T(8,128)(2,1)}, u32[]{:S(2)}) copy-start(bf16[8192,128]{1,0:T(8,128)(2,1)} %get-tuple-element.648) | copy-start | bytes 6291460 | tf_op jit(solution)/shard_map/while
  312.3 2.1 copy-start.1
  313.0 1.4 copy-start.8
  318.8 1.9 copy-start.4
  320.7 1.0 copy-start.7
  332.4 40.9 %copy-start.5 = (bf16[1,16,8192]{2,1,0:T(8,128)(2,1)S(1)}, bf16[1,16,8192]{2,1,0:T(8,128)(2,1)}, u32[]{:S(2)}) copy-start(bf16[1,16,8192]{2,1,0:T(8,128)(2,1)} %get-tuple-element.624) | copy-start | bytes 786436 | tf_op jit(solution)/shard_map/while
  375.1 0.7 copy-start.6
  375.8 15.4 %copy-start.3 = (bf16[4224,128]{0,1:T(8,128)(2,1)}, bf16[4224,128]{0,1:T(8,128)(2,1)S(1)}, u32[]{:S(2)}) copy-start(bf16[4224,128]{0,1:T(8,128)(2,1)S(1)} %get-tuple-element.622) | copy-start | bytes 3244036 | tf_op jit(solution)/shard_map/while
  375.8 42.3 %all-gather.2.cloned.1.call-start = ((), (), s32[]{:S(2)}) async-start(), calls=%async_computation.1 | async-start | bytes 2359296 | tf_op jit(solution)/shard_map/while/body/eval_jaxpr/all_gather | solution.py:142
  376.9 9.0 %collective-permute-start = (bf16[16,8192]{1,0:T(8,128)(2,1)S(1)}, bf16[16,8192]{1,0:T(8,128)(2,1)S(1)}, u32[]{:S(2)}, u32[]{:S(2)}) collective-permute-start(bf16[16,8192]{1,0:T(8,128)(2,1)S(1)} %broadcast_select_fusion.2), channel_id=1, source_target_pairs={{0,8},{8,16},{16,24},{1,9},{9,17},{17,25},{2,10},{10,18},{18,26},{... | collective-permute-start | bytes 786440 | tf_op jit(solution)/shard_map/while/body/eval_jaxpr/ppermute | solution.py:39
  388.7 106.3 %reduce-scatter.2.cloned.1.call-start = ((), (), s32[]{:S(2)}) async-start(), calls=%async_computation.2 | async-start | bytes 2359296 | tf_op jit(solution)/shard_map/while/body/eval_jaxpr/reduce_scatter | solution.py:190
  418.1 5.0 copy-start
  423.1 9.1 %copy-start.2 = (bf16[8192,128]{1,0:T(8,128)(2,1)S(1)}, bf16[8192,128]{1,0:T(8,128)(2,1)}, u32[]{:S(2)}) copy-start(bf16[8192,128]{1,0:T(8,128)(2,1)} %get-tuple-element.648) | copy-start | bytes 6291460 | tf_op jit(solution)/shard_map/while
  434.0 2.1 copy-start.1
  434.8 1.4 copy-start.8
  440.6 1.9 copy-start.4
  442.4 1.0 copy-start.7
  454.1 40.9 %copy-start.5 = (bf16[1,16,8192]{2,1,0:T(8,128)(2,1)S(1)}, bf16[1,16,8192]{2,1,0:T(8,128)(2,1)}, u32[]{:S(2)}) copy-start(bf16[1,16,8192]{2,1,0:T(8,128)(2,1)} %get-tuple-element.624) | copy-start | bytes 786436 | tf_op jit(solution)/shard_map/while
  496.9 0.7 copy-start.6
Sparse Core Ops, SparseCore 0:
  22.6 30.1 all-gather.1
  88.9 40.7 reduce-scatter.1
  145.3 29.2 all-gather.1
  210.7 40.7 reduce-scatter.1
  267.1 29.2 all-gather.1
  332.5 40.7 reduce-scatter.1
  388.9 29.1 all-gather.1
  454.2 40.7 reduce-scatter.1
where the time goes:
time: 508 us; the launch traced here: 504 us
  waiting for transfers between devices  282 us (56%)
  matrix products  103 us (20%)
  local copies, waits for them, and re-layouts  59.2 us (12%)
  other arithmetic  40.5 us (8%)
  between operations  13.4 us (3%)
  starting transfers between devices  5.35 us (1%)
    reduce_scatter x4, waiting for transfers between devices, step(): lax.psum_scatter(jnp.dot(attended, out_matrix, preferred_element_type=jnp...  153 us
    all_gather x4, waiting for transfers between devices, step(): projected = project(lax.all_gather(normed, 'head', axis=0, tiled=True))  97.2 us
    dot_general x4, matrix products, step(): jnp.dot(attended, out_matrix, preferred_element_type=jnp.float32)  38.3 us
    dot_general x4, matrix products, project(): jnp.dot(rows_piece, query_matrix, preferred_element_type=jnp.float32)  33 us
    ppermute x4, waiting for transfers between devices, from_behind(): lax.ppermute(value, axis, [(source, source + steps) for source in range(f...  31 us
    while x92, local copies, waits for them, and re-layouts  30.3 us
    dot_general x4, matrix products, project(): jnp.dot(rows_piece, key_matrix, preferred_element_type=jnp.float32)  13.2 us
  transfers between devices with their start and end apart: 12, of which 12 were waited for; matrix products, arithmetic and copies ran while one was open for 6% of the time, Pallas kernels for 0%

commit v1 on v0

v1 whole, which is shorter than its diff:
```python
import functools
import math

import jax
import jax.numpy as jnp
from jax import lax
from jax.experimental import pallas as pl
from jax.experimental.pallas import tpu as pltpu
from jax.sharding import PartitionSpec as P

HD = 128
BLOCK = 128
EPS = 1e-05
THETA = 500000.0
CHUNKS = 8
MASKED = -1e30


def exchange(value, distance):
    count = lax.axis_size("head")
    return lax.ppermute(value, "head", [(i, i ^ distance) for i in range(count)])


def forward(value, section):
    return lax.ppermute(value, "section", [(section - 1, section)])


def join_columns(part, group_bits, head_index):
    for bit in range(group_bits):
        other = exchange(part, 1 << bit)
        is_lower = head_index >> bit & 1 == 0
        part = jnp.where(
            is_lower, jnp.concatenate([part, other], -1), jnp.concatenate([other, part], -1)
        )
    return part


def layer_kernel(
    piece_count,
    cached_blocks,
    lists_ref,
    *refs,
):
    pieces = refs[:piece_count]
    (wq_hbm, wk_hbm, wv_hbm, wo_hbm, keys_hbm, values_hbm) = refs[piece_count : piece_count + 6]
    cos_ref, sin_ref, row_ref, col_ref = refs[piece_count + 6 : piece_count + 10]
    outs = refs[piece_count + 10 : 2 * piece_count + 10]
    (x_s, wq_s, wk_s, wv_s, wo_s, k_s, v_s, q_s, kv_s, att_s, sem_q, sem_kv, sem_o, sem_c) = refs[
        2 * piece_count + 10 :
    ]
    tokens = x_s.shape[1]
    depth = x_s.shape[2]
    rows = pieces[0].shape[0]
    query_cols = wq_s.shape[2]
    out_cols = wo_s.shape[2]
    query_heads = query_cols // HD
    listed = k_s.shape[0] // BLOCK

    def query_copy(k):
        return pltpu.make_async_copy(
            wq_hbm.at[0, pl.ds(k * depth, depth), :], wq_s.at[k], sem_q.at[k]
        )

    def key_copy():
        return pltpu.make_async_copy(wk_hbm.at[0], wk_s, sem_kv.at[0])

    def value_copy():
        return pltpu.make_async_copy(wv_hbm.at[0], wv_s, sem_kv.at[1])

    def out_copy(n):
        return pltpu.make_async_copy(
            wo_hbm.at[0, :, pl.ds(n * out_cols, out_cols)], wo_s.at[n], sem_o.at[n]
        )

    cache_copies = []
    passed = lists_ref[0, 0] == cached_blocks
    for j in range(listed - 1):
        if j:
            passed = passed | (lists_ref[0, j] == cached_blocks)
        block = jnp.where(passed, lists_ref[0, j + 1], lists_ref[0, j])
        block = jnp.clip(block, 0, cached_blocks - 1)
        start = pl.multiple_of(block * BLOCK, BLOCK)
        for which, (source, target) in enumerate(((keys_hbm, k_s), (values_hbm, v_s))):
            cache_copies.append(
                pltpu.make_async_copy(
                    source.at[0, pl.ds(start, BLOCK), :],
                    target.at[pl.ds(j * BLOCK, BLOCK), :],
                    sem_c.at[which, j],
                )
            )

    key_copy().start()
    value_copy().start()
    for k in range(CHUNKS):
        query_copy(k).start()
    for copy in cache_copies:
        copy.start()
    for n in range(CHUNKS):
        out_copy(n).start()

    for k in range(CHUNKS):
        for p, piece in enumerate(pieces):
            x_s[k, p * rows : (p + 1) * rows, :] = piece[:, k * depth : (k + 1) * depth]

    key_copy().wait()
    value_copy().wait()

    def project(k, carry):
        query_copy(k).wait()
        x = x_s[k]
        start = pl.multiple_of(k * depth, depth)
        q_new = jnp.dot(x, wq_s[k], preferred_element_type=jnp.float32)
        k_new = jnp.dot(x, wk_s[pl.ds(start, depth), :], preferred_element_type=jnp.float32)
        v_new = jnp.dot(x, wv_s[pl.ds(start, depth), :], preferred_element_type=jnp.float32)

        @pl.when(k == 0)
        def _():
            q_s[...] = q_new
            kv_s[0] = k_new
            kv_s[1] = v_new

        @pl.when(k != 0)
        def _():
            q_s[...] += q_new
            kv_s[0] += k_new
            kv_s[1] += v_new

        return carry

    lax.fori_loop(0, CHUNKS, project, 0)

    cosine, sine = cos_ref[...], sin_ref[...]

    def rotated(value):
        return (value * cosine + pltpu.roll(value, HD // 2, 1) * sine).astype(jnp.bfloat16)

    k_s[(listed - 1) * BLOCK :, :] = rotated(kv_s[0].astype(jnp.bfloat16).astype(jnp.float32))
    v_s[(listed - 1) * BLOCK :, :] = kv_s[1].astype(jnp.bfloat16)
    for copy in cache_copies:
        copy.wait()
    keys, values = k_s[...], v_s[...]
    allowed = col_ref[...] <= row_ref[...]
    factor = math.log2(math.e) / math.sqrt(HD)
    for head in range(query_heads):
        columns = slice(head * HD, (head + 1) * HD)
        query = rotated(q_s[:, columns])
        scores = lax.dot_general(
            query, keys, (((1,), (1,)), ((), ())), preferred_element_type=jnp.float32
        )
        scores = jnp.concatenate(
            [
                scores[:, : (listed - 1) * BLOCK],
                jnp.where(allowed, scores[:, (listed - 1) * BLOCK :], MASKED),
            ],
            1,
        )
        peak = jnp.max(scores, -1, keepdims=True)
        probabilities = jnp.exp2((scores - peak) * factor)
        totals = jnp.sum(probabilities, -1, keepdims=True)
        mixed = jnp.dot(
            probabilities.astype(jnp.bfloat16), values, preferred_element_type=jnp.float32
        )
        att_s[:, columns] = (mixed / totals).astype(jnp.bfloat16)

    def give(n, carry):
        out_copy(n).wait()
        result = jnp.dot(att_s[...], wo_s[n], preferred_element_type=jnp.float32)
        result = result.astype(jnp.bfloat16)
        columns = pl.ds(pl.multiple_of(n * out_cols, out_cols), out_cols)
        for p, out in enumerate(outs):
            out[:, columns] = result[p * rows : (p + 1) * rows]
        return carry

    lax.fori_loop(0, CHUNKS, give, 0)


def layer(pieces, weights, cache, lists, tables):
    query_weight, key_weight, value_weight, out_weight = weights
    width = query_weight.shape[1]
    query_cols = query_weight.shape[2]
    listed = lists.shape[1]
    rows = pieces[0].shape[0]
    tokens = rows * len(pieces)
    depth, out_cols = width // CHUNKS, out_weight.shape[2] // CHUNKS
    vmem = pl.BlockSpec(memory_space=pltpu.VMEM)
    anywhere = pl.BlockSpec(memory_space=pl.ANY)
    size = 2 * (width * (query_cols + 2 * HD) + query_cols * out_weight.shape[2])
    return pl.pallas_call(
        functools.partial(layer_kernel, len(pieces), cache[0].shape[1] // BLOCK),
        out_shape=[jax.ShapeDtypeStruct((rows, out_weight.shape[2]), jnp.bfloat16)] * len(pieces),
        in_specs=[pl.BlockSpec(memory_space=pltpu.SMEM)]
        + [vmem] * len(pieces)
        + [anywhere] * 6
        + [vmem] * 4,
        out_specs=[vmem] * len(pieces),
        scratch_shapes=[
            pltpu.VMEM((CHUNKS, tokens, depth), jnp.bfloat16),
            pltpu.VMEM((CHUNKS, depth, query_cols), jnp.bfloat16),
            pltpu.VMEM((width, HD), jnp.bfloat16),
            pltpu.VMEM((width, HD), jnp.bfloat16),
            pltpu.VMEM((CHUNKS, query_cols, out_cols), jnp.bfloat16),
            pltpu.VMEM((listed * BLOCK, HD), jnp.bfloat16),
            pltpu.VMEM((listed * BLOCK, HD), jnp.bfloat16),
            pltpu.VMEM((tokens, query_cols), jnp.float32),
            pltpu.VMEM((2, tokens, HD), jnp.float32),
            pltpu.VMEM((tokens, query_cols), jnp.bfloat16),
            pltpu.SemaphoreType.DMA((CHUNKS,)),
            pltpu.SemaphoreType.DMA((2,)),
            pltpu.SemaphoreType.DMA((CHUNKS,)),
            pltpu.SemaphoreType.DMA((2, listed - 1)),
        ],
        compiler_params=pltpu.CompilerParams(vmem_limit_bytes=52 << 20),
        cost_estimate=pl.CostEstimate(
            flops=tokens * size, bytes_accessed=size, transcendentals=tokens * listed * BLOCK * 8
        ),
        name="attention_sublayer",
    )(lists, *pieces, *weights, *cache, *tables)


def gather_rows(own):
    count = lax.axis_size("head")
    pieces = [own if not j else exchange(own, j) for j in range(0, count, 2)]
    return [p for piece in pieces for p in (piece, exchange(piece, 1))]


def scatter_rows(partials):
    count = lax.axis_size("head")
    terms = []
    for j in reversed(range(0, count, 2)):
        both = partials[j].astype(jnp.float32) + exchange(partials[j + 1], 1).astype(jnp.float32)
        both = both.astype(jnp.bfloat16)
        terms.append(exchange(both, j) if j else both)
    return terms


def on_device(
    prompt_states,
    norm_gain,
    query_weight,
    key_weight,
    value_weight,
    out_weight,
    cache_keys,
    cache_values,
    block_lists,
):
    sections = lax.axis_size("section")
    heads = lax.axis_size("head")
    section_index = lax.axis_index("section")
    head_index = lax.axis_index("head")
    rows = prompt_states.shape[1]
    tokens = rows * heads
    prefix = cache_keys.shape[1]
    group_bits = (HD // key_weight.shape[2]).bit_length() - 1
    weights = (
        query_weight,
        join_columns(key_weight, group_bits, head_index),
        join_columns(value_weight, group_bits, head_index),
        out_weight,
    )
    cache = (
        join_columns(cache_keys, group_bits, head_index),
        join_columns(cache_values, group_bits, head_index),
    )
    gain_row = norm_gain[0]

    whole_tiles = rows % 16 == 0
    block_of = jnp.arange(heads, dtype=jnp.int32) ^ head_index
    positions = (
        prefix + block_of[:, None] * rows + jnp.arange(rows, dtype=jnp.int32)[None, :]
    ).reshape(tokens)
    inverse_freq = jnp.exp(-math.log(THETA) * jnp.arange(HD // 2, dtype=jnp.float32) * 2.0 / HD)
    angles = positions.astype(jnp.float32)[:, None] * inverse_freq[None, :]
    cosine, sine = jnp.cos(angles), jnp.sin(angles)
    tables = (
        jnp.concatenate([cosine, cosine], 1),
        jnp.concatenate([-sine, sine], 1),
        positions[:, None],
        positions[None, :],
    )

    states = prompt_states[0]
    output = jnp.zeros_like(states)
    for step in range(sections):
        if step:
            states = forward(states, step)
        widened = states.astype(jnp.float32)
        normed = (
            widened * lax.rsqrt(jnp.mean(widened * widened, -1, keepdims=True) + EPS) * gain_row
        ).astype(jnp.bfloat16)
        pieces = gather_rows(normed)
        if not whole_tiles:
            pieces = [jnp.concatenate(pieces, 0)]
        partials = layer(pieces, weights, cache, block_lists, tables)
        if not whole_tiles:
            partials = jnp.split(partials[0], heads, 0)
        summed = sum(term.astype(jnp.float32) for term in scatter_rows(partials))
        states = (widened + summed).astype(jnp.bfloat16)
        output = jnp.where(section_index == step, states, output)
    return output[None, None]


def solution(mesh):
    return jax.shard_map(
        on_device,
        mesh=mesh,
        in_specs=(
            P(None, "head", None),
            P("section", None),
            P("section", None, "head"),
            P("section", None, "head"),
            P("section", None, "head"),
            P("section", "head", None),
            P("section", None, "head"),
            P("section", None, "head"),
            P(),
        ),
        out_specs=P("section", None, "head", None),
        check_vma=False,
    )
```

time: 508 us -> 274 us (0.54)
  waiting for transfers between devices: 282 us -> 88.7 us
  matrix products: 103 us -> 0 us
  Pallas kernels: 0 us -> 101 us
  starting transfers between devices: 5.35 us -> 68 us
  local copies, waits for them, and re-layouts: 59.2 us -> 4.66 us
  other arithmetic: 40.5 us -> 9.92 us
  between operations: 13.4 us -> 0.48 us
    reduce_scatter x4 -> x0, waiting for transfers between devices: 153 us -> none  [step(): lax.psum_scatter(jnp.dot(attended, out_matrix, preferred_element_type=jnp...]
    dot_general x24 -> x0, matrix products: 103 us -> none  [the longest x4 38.3 us: step(): jnp.dot(attended, out_matrix, preferred_element_type=jnp.float32)]
    pallas_call x0 -> x4, Pallas kernels: none -> 101 us  [layer(): pl.pallas_call(functools.partial(layer_kernel, len(pieces), cache[0].shap...]
    all_gather x4 -> x0, waiting for transfers between devices: 97.2 us -> none  [step(): projected = project(lax.all_gather(normed, 'head', axis=0, tiled=True))]
    ppermute x4 -> x59, starting transfers between devices: 5.17 us -> 68 us  [the longest x56 65.1 us: exchange(): lax.ppermute(value, 'head', [(i, i ^ distance) for i in range(count)])]
    ppermute x4 -> x59, waiting for transfers between devices: 31 us -> 88.7 us  [the longest x56 67.1 us: exchange(): lax.ppermute(value, 'head', [(i, i ^ distance) for i in range(count)])]
    while x92 -> x0, local copies, waits for them, and re-layouts: 30.3 us -> none
    gather x8 -> x0, local copies, waits for them, and re-layouts: 10.2 us -> none  [the longest x4 5.12 us: step(): key_store.reshape(-1, BLOCK, HD)[block_lists]]
  transfers between devices with their start and end apart: 12 -> 59, of which waited for: 12 -> 25; matrix products, arithmetic and copies ran while one was open for 6% -> 2% of each run, Pallas kernels for 0% -> 0%
where the time goes in v1:
time: 274 us; the launch traced here: 273 us
  Pallas kernels  101 us (37%)
  waiting for transfers between devices  88.7 us (32%)
  starting transfers between devices  68 us (25%)
  other arithmetic  9.92 us (4%)
  local copies, waits for them, and re-layouts  4.66 us (2%)
    pallas_call x4, Pallas kernels, layer(): pl.pallas_call(functools.partial(layer_kernel, len(pieces), cache[0].shap...  101 us
    ppermute x56, waiting for transfers between devices, exchange(): lax.ppermute(value, 'head', [(i, i ^ distance) for i in range(count)])  67.1 us
    ppermute x56, starting transfers between devices, exchange(): lax.ppermute(value, 'head', [(i, i ^ distance) for i in range(count)])  65.1 us
    ppermute x3, waiting for transfers between devices, forward(): return lax.ppermute(value, 'section', [(section - 1, section)])  21.7 us
  transfers between devices with their start and end apart: 59, of which 25 were waited for; matrix products, arithmetic and copies ran while one was open for 2% of the time, Pallas kernels for 0%

profile of v1, /device:TPU:25, one launch (start us, length us, event | category | flops | bytes accessed | tf_op | source)
XLA Modules:
  0.0 273.2 jit_solution(655408478755325216)
XLA Ops:
  0.0 1.1 fusion.12
  1.1 1.1 fusion.14.refs_0_
  2.2 1.3 collective-permute-start.1
  3.5 1.2 collective-permute-start.3
  5.0 1.5 collective-permute-start
  6.8 2.7 collective-permute-done.1.refs_2_
  9.5 2.7 collective-permute-start.2
  12.2 5.7 %collective-permute-start.4 = (bf16[16,8192]{1,0:T(8,128)(2,1)S(1)}, bf16[16,8192]{1,0:T(8,128)(2,1)S(1)}, u32[]{:S(2)}, u32[]{:S(2)}) collective-permute-start(bf16[16,8192]{1,0:T(8,128)(2,1)S(1)} %collective-permute-done.3.refs_4_), channel_id=1, source_target_pairs={{0,1},{1,0},{2,3},{3,2},{4,5},{5,4},{6,7},{7,6},{8,9},{9,8},{10,11... | collective-permute-start | bytes 786440 | tf_op jit(solution)/shard_map/ppermute | solution.py:21
  20.8 25.4 %attention_sublayer.4 = (bf16[16,8192]{1,0:T(8,128)(2,1)S(1)}, bf16[16,8192]{1,0:T(8,128)(2,1)S(1)}, bf16[16,8192]{1,0:T(8,128)(2,1)S(1)}, bf16[16,8192]{1,0:T(8...) custom-call(s32[1,8]{1,0:T(1,128)S(1)} %copy-done, ...), custom_call_target="tpu_custom_call" | custom-call | flops 4831838208 | bytes 37748736 | tf_op jit(solution)/shard_map/attention_sublayer/pallas_call | solution.py:188
  47.3 0.7 collective-permute-done.7
  48.0 1.0 add_convert_fusion.15
  49.0 1.3 collective-permute-start.8
  51.0 1.0 collective-permute-start.12
  52.0 5.5 %collective-permute-done.8 = bf16[16,8192]{1,0:T(8,128)(2,1)S(1)} collective-permute-done((bf16[16,8192]{1,0:T(8,128)(2,1)S(1)}, bf16[16,8192]{1,0:T(8,128)(2,1)S(1)}, u32[]{:S(2)}, u32[]{:S(2)}) %collective-permute-start.8) | collective-permute-done | bytes 262176 | tf_op jit(solution)/shard_map/ppermute | solution.py:21
  57.5 6.3 %collective-permute-done.10 = bf16[16,8192]{1,0:T(8,128)(2,1)S(1)} collective-permute-done((bf16[16,8192]{1,0:T(8,128)(2,1)S(1)}, bf16[16,8192]{1,0:T(8,128)(2,1)S(1)}, u32[]{:S(2)}, u32[]{:S(2)}) %collective-permute-start.10) | collective-permute-done | bytes 262176 | tf_op jit(solution)/shard_map/ppermute | solution.py:21
  65.7 0.9 collective-permute-start.18
  66.7 1.1 collective-permute-start.20
  67.8 1.4 collective-permute-start.15
  69.2 3.2 %collective-permute-done.16.refs_2_ = bf16[16,8192]{1,0:T(8,128)(2,1)S(1)} collective-permute-done((bf16[16,8192]{1,0:T(8,128)(2,1)S(1)}, bf16[16,8192]{1,0:T(8,128)(2,1)S(1)}, u32[]{:S(2)}, u32[]{:S(2)}) %collective-permute-start.16) | collective-permute-done | bytes 262176 | tf_op jit(solution)/shard_map/ppermute | solution.py:21
  72.4 2.5 collective-permute-start.17
  74.9 5.1 %collective-permute-start.19 = (bf16[16,8192]{1,0:T(8,128)(2,1)S(1)}, bf16[16,8192]{1,0:T(8,128)(2,1)S(1)}, u32[]{:S(2)}, u32[]{:S(2)}) collective-permute-start(bf16[16,8192]{1,0:T(8,128)(2,1)S(1)} %collective-permute-done.18.refs_4_), channel_id=1, source_target_pairs={{0,1},{1,0},{2,3},{3,2},{4,5},{5,4},{6,7},{7,6},{8,9},{9,8},{10,11... | collective-permute-start | bytes 786440 | tf_op jit(solution)/shard_map/ppermute | solution.py:21
  80.2 1.1 collective-permute-done.19.refs_5_
  82.6 25.4 %attention_sublayer.5 = (bf16[16,8192]{1,0:T(8,128)(2,1)S(1)}, bf16[16,8192]{1,0:T(8,128)(2,1)S(1)}, bf16[16,8192]{1,0:T(8,128)(2,1)S(1)}, bf16[16,8192]{1,0:T(8...) custom-call(s32[1,8]{1,0:T(1,128)S(1)} %copy-done, ...), custom_call_target="tpu_custom_call" | custom-call | flops 4831838208 | bytes 37748736 | tf_op jit(solution)/shard_map/attention_sublayer/pallas_call | solution.py:188
  109.1 0.7 collective-permute-done.22
  109.8 1.0 add_convert_fusion.11
  110.8 1.4 collective-permute-start.23
  112.3 0.8 collective-permute-start.25
  113.8 5.5 %collective-permute-done.23 = bf16[16,8192]{1,0:T(8,128)(2,1)S(1)} collective-permute-done((bf16[16,8192]{1,0:T(8,128)(2,1)S(1)}, bf16[16,8192]{1,0:T(8,128)(2,1)S(1)}, u32[]{:S(2)}, u32[]{:S(2)}) %collective-permute-start.23) | collective-permute-done | bytes 262176 | tf_op jit(solution)/shard_map/ppermute | solution.py:21
  119.4 6.3 %collective-permute-done.25 = bf16[16,8192]{1,0:T(8,128)(2,1)S(1)} collective-permute-done((bf16[16,8192]{1,0:T(8,128)(2,1)S(1)}, bf16[16,8192]{1,0:T(8,128)(2,1)S(1)}, u32[]{:S(2)}, u32[]{:S(2)}) %collective-permute-start.25) | collective-permute-done | bytes 262176 | tf_op jit(solution)/shard_map/ppermute | solution.py:21
  125.9 0.9 collective-permute-start.29
  127.1 1.0 collective-permute-start.31
  128.1 0.8 collective-permute-start.33
  128.8 1.0 collective-permute-start.35
  129.8 1.3 collective-permute-start.30
  131.1 3.4 %collective-permute-done.31.refs_2_ = bf16[16,8192]{1,0:T(8,128)(2,1)S(1)} collective-permute-done((bf16[16,8192]{1,0:T(8,128)(2,1)S(1)}, bf16[16,8192]{1,0:T(8,128)(2,1)S(1)}, u32[]{:S(2)}, u32[]{:S(2)}) %collective-permute-start.31) | collective-permute-done | bytes 262176 | tf_op jit(solution)/shard_map/ppermute | solution.py:21
  134.5 2.3 collective-permute-start.32
  136.8 5.6 %collective-permute-start.34 = (bf16[16,8192]{1,0:T(8,128)(2,1)S(1)}, bf16[16,8192]{1,0:T(8,128)(2,1)S(1)}, u32[]{:S(2)}, u32[]{:S(2)}) collective-permute-start(bf16[16,8192]{1,0:T(8,128)(2,1)S(1)} %collective-permute-done.33.refs_4_), channel_id=1, source_target_pairs={{0,1},{1,0},{2,3},{3,2},{4,5},{5,4},{6,7},{7,6},{8,9},{9,8},{10,11... | collective-permute-start | bytes 786440 | tf_op jit(solution)/shard_map/ppermute | solution.py:21
  142.5 1.1 collective-permute-done.34.refs_5_
  145.0 25.4 %attention_sublayer.6 = (bf16[16,8192]{1,0:T(8,128)(2,1)S(1)}, bf16[16,8192]{1,0:T(8,128)(2,1)S(1)}, bf16[16,8192]{1,0:T(8,128)(2,1)S(1)}, bf16[16,8192]{1,0:T(8...) custom-call(s32[1,8]{1,0:T(1,128)S(1)} %copy-done, ...), custom_call_target="tpu_custom_call" | custom-call | flops 4831838208 | bytes 37748736 | tf_op jit(solution)/shard_map/attention_sublayer/pallas_call | solution.py:188
  171.4 0.7 collective-permute-done.37
  172.2 1.0 add_convert_fusion.7
  173.2 1.3 collective-permute-start.38
  175.2 1.0 collective-permute-start.42
  176.2 5.5 %collective-permute-done.38 = bf16[16,8192]{1,0:T(8,128)(2,1)S(1)} collective-permute-done((bf16[16,8192]{1,0:T(8,128)(2,1)S(1)}, bf16[16,8192]{1,0:T(8,128)(2,1)S(1)}, u32[]{:S(2)}, u32[]{:S(2)}) %collective-permute-start.38) | collective-permute-done | bytes 262176 | tf_op jit(solution)/shard_map/ppermute | solution.py:21
  181.7 6.3 %collective-permute-done.40 = bf16[16,8192]{1,0:T(8,128)(2,1)S(1)} collective-permute-done((bf16[16,8192]{1,0:T(8,128)(2,1)S(1)}, bf16[16,8192]{1,0:T(8,128)(2,1)S(1)}, u32[]{:S(2)}, u32[]{:S(2)}) %collective-permute-start.40) | collective-permute-done | bytes 262176 | tf_op jit(solution)/shard_map/ppermute | solution.py:21
  188.2 1.3 collective-permute-start.44
  189.5 21.7 %collective-permute-done.44 = bf16[16,8192]{1,0:T(8,128)(2,1)S(1)} collective-permute-done((bf16[16,8192]{1,0:T(8,128)(2,1)S(1)}, bf16[16,8192]{1,0:T(8,128)(2,1)S(1)}, u32[]{:S(2)}, u32[]{:S(2)}) %collective-permute-start.44) | collective-permute-done | bytes 262176 | tf_op jit(solution)/shard_map/ppermute | solution.py:25
  211.5 0.8 collective-permute-start.46
  212.3 0.9 collective-permute-start.48
  213.2 1.0 collective-permute-start.50
  214.2 1.9 collective-permute-start.45
  216.1 2.3 collective-permute-done.46.refs_2_
  218.4 3.5 %collective-permute-start.47 = (bf16[16,8192]{1,0:T(8,128)(2,1)S(1)}, bf16[16,8192]{1,0:T(8,128)(2,1)S(1)}, u32[]{:S(2)}, u32[]{:S(2)}) collective-permute-start(bf16[16,8192]{1,0:T(8,128)(2,1)S(1)} %collective-permute-done.46.refs_2_), channel_id=1, source_target_pairs={{0,1},{1,0},{2,3},{3,2},{4,5},{5,4},{6,7},{7,6},{8,9},{9,8},{10,11... | collective-permute-start | bytes 786440 | tf_op jit(solution)/shard_map/ppermute | solution.py:21
  221.8 4.8 %collective-permute-start.49 = (bf16[16,8192]{1,0:T(8,128)(2,1)S(1)}, bf16[16,8192]{1,0:T(8,128)(2,1)S(1)}, u32[]{:S(2)}, u32[]{:S(2)}) collective-permute-start(bf16[16,8192]{1,0:T(8,128)(2,1)S(1)} %collective-permute-done.48.refs_4_), channel_id=1, source_target_pairs={{0,1},{1,0},{2,3},{3,2},{4,5},{5,4},{6,7},{7,6},{8,9},{9,8},{10,11... | collective-permute-start | bytes 786440 | tf_op jit(solution)/shard_map/ppermute | solution.py:21
  226.7 1.1 collective-permute-done.49.refs_5_
  229.2 25.4 %attention_sublayer.7 = (bf16[16,8192]{1,0:T(8,128)(2,1)S(1)}, bf16[16,8192]{1,0:T(8,128)(2,1)S(1)}, bf16[16,8192]{1,0:T(8,128)(2,1)S(1)}, bf16[16,8192]{1,0:T(8...) custom-call(s32[1,8]{1,0:T(1,128)S(1)} %copy-done, ...), custom_call_target="tpu_custom_call" | custom-call | flops 4831838208 | bytes 37748736 | tf_op jit(solution)/shard_map/attention_sublayer/pallas_call | solution.py:188
  255.6 0.7 collective-permute-done.52
  256.4 1.0 add_convert_fusion.3
  257.4 1.1 collective-permute-start.53
  258.5 1.0 collective-permute-start.55
  259.6 0.8 collective-permute-start.57
  260.4 5.5 %collective-permute-done.53 = bf16[16,8192]{1,0:T(8,128)(2,1)S(1)} collective-permute-done((bf16[16,8192]{1,0:T(8,128)(2,1)S(1)}, bf16[16,8192]{1,0:T(8,128)(2,1)S(1)}, u32[]{:S(2)}, u32[]{:S(2)}) %collective-permute-start.53) | collective-permute-done | bytes 262176 | tf_op jit(solution)/shard_map/ppermute | solution.py:21
  265.9 6.3 %collective-permute-done.55 = bf16[16,8192]{1,0:T(8,128)(2,1)S(1)} collective-permute-done((bf16[16,8192]{1,0:T(8,128)(2,1)S(1)}, bf16[16,8192]{1,0:T(8,128)(2,1)S(1)}, u32[]{:S(2)}, u32[]{:S(2)}) %collective-permute-start.55) | collective-permute-done | bytes 262176 | tf_op jit(solution)/shard_map/ppermute | solution.py:21
  272.2 1.0 fusion.17
  (164 shorter events, 17.5 us)
Async XLA Ops:
  2.2 17.2 %copy-start.2 = (bf16[16,8192]{1,0:T(8,128)(2,1)}, bf16[16,8192]{1,0:T(8,128)(2,1)S(1)}, u32[]{:S(2)}) copy-start(bf16[16,8192]{1,0:T(8,128)(2,1)S(1)} %fusion.14.refs_0_) | copy-start | bytes 786436
  2.2 7.2 %collective-permute-start.1 = (bf16[16,8192]{1,0:T(8,128)(2,1)S(1)}, bf16[16,8192]{1,0:T(8,128)(2,1)S(1)}, u32[]{:S(2)}, u32[]{:S(2)}) collective-permute-start(bf16[16,8192]{1,0:T(8,128)(2,1)S(1)} %fusion.14.refs_0_), channel_id=1, source_target_pairs={{0,2},{1,3},{2,0},{3,1},{4,6},{5,7},{6,4},{7,5},{8,10},{9,11},{10,... | collective-permute-start | bytes 786440 | tf_op jit(solution)/shard_map/ppermute | solution.py:21
  3.5 8.7 %collective-permute-start.3 = (bf16[16,8192]{1,0:T(8,128)(2,1)S(1)}, bf16[16,8192]{1,0:T(8,128)(2,1)S(1)}, u32[]{:S(2)}, u32[]{:S(2)}) collective-permute-start(bf16[16,8192]{1,0:T(8,128)(2,1)S(1)} %fusion.14.refs_0_), channel_id=1, source_target_pairs={{0,4},{1,5},{2,6},{3,7},{4,0},{5,1},{6,2},{7,3},{8,12},{9,13},{10,... | collective-permute-start | bytes 786440 | tf_op jit(solution)/shard_map/ppermute | solution.py:21
  4.8 13.1 %collective-permute-start.5 = (bf16[16,8192]{1,0:T(8,128)(2,1)S(1)}, bf16[16,8192]{1,0:T(8,128)(2,1)S(1)}, u32[]{:S(2)}, u32[]{:S(2)}) collective-permute-start(bf16[16,8192]{1,0:T(8,128)(2,1)S(1)} %fusion.14.refs_0_), channel_id=1, source_target_pairs={{0,6},{1,7},{2,4},{3,5},{4,2},{5,3},{6,0},{7,1},{8,14},{9,15},{10,... | collective-permute-start | bytes 786440 | tf_op jit(solution)/shard_map/ppermute | solution.py:21
  5.0 13.4 %collective-permute-start = (bf16[16,8192]{1,0:T(8,128)(2,1)S(1)}, bf16[16,8192]{1,0:T(8,128)(2,1)S(1)}, u32[]{:S(2)}, u32[]{:S(2)}) collective-permute-start(bf16[16,8192]{1,0:T(8,128)(2,1)S(1)} %fusion.14.refs_0_), channel_id=1, source_target_pairs={{0,1},{1,0},{2,3},{3,2},{4,5},{5,4},{6,7},{7,6},{8,9},{9,8},{10,11... | collective-permute-start | bytes 786440 | tf_op jit(solution)/shard_map/ppermute | solution.py:21
  9.5 8.9 %collective-permute-start.2 = (bf16[16,8192]{1,0:T(8,128)(2,1)S(1)}, bf16[16,8192]{1,0:T(8,128)(2,1)S(1)}, u32[]{:S(2)}, u32[]{:S(2)}) collective-permute-start(bf16[16,8192]{1,0:T(8,128)(2,1)S(1)} %collective-permute-done.1.refs_2_), channel_id=1, source_target_pairs={{0,1},{1,0},{2,3},{3,2},{4,5},{5,4},{6,7},{7,6},{8,9},{9,8},{10,11... | collective-permute-start | bytes 786440 | tf_op jit(solution)/shard_map/ppermute | solution.py:21
  12.2 6.8 %collective-permute-start.4 = (bf16[16,8192]{1,0:T(8,128)(2,1)S(1)}, bf16[16,8192]{1,0:T(8,128)(2,1)S(1)}, u32[]{:S(2)}, u32[]{:S(2)}) collective-permute-start(bf16[16,8192]{1,0:T(8,128)(2,1)S(1)} %collective-permute-done.3.refs_4_), channel_id=1, source_target_pairs={{0,1},{1,0},{2,3},{3,2},{4,5},{5,4},{6,7},{7,6},{8,9},{9,8},{10,11... | collective-permute-start | bytes 786440 | tf_op jit(solution)/shard_map/ppermute | solution.py:21
  17.9 1.5 collective-permute-start.6
  20.8 43.1 %copy-start.1 = (bf16[1,16,8192]{2,1,0:T(8,128)(2,1)S(1)}, bf16[1,16,8192]{2,1,0:T(8,128)(2,1)}, u32[]{:S(2)}) copy-start(bf16[1,16,8192]{2,1,0:T(8,128)(2,1)} %param.9) | copy-start | bytes 786436
  20.8 44.2 %copy-start.6 = (f32[1,8192]{1,0:T(1,128)S(1)}, f32[1,8192]{1,0:T(1,128)}, u32[]{:S(2)}) copy-start(f32[1,8192]{1,0:T(1,128)} %param.10) | copy-start | bytes 98308
  46.2 1.8 collective-permute-start.7
  46.6 3.7 %collective-permute-start.9 = (bf16[16,8192]{1,0:T(8,128)(2,1)S(1)}, bf16[16,8192]{1,0:T(8,128)(2,1)S(1)}, u32[]{:S(2)}, u32[]{:S(2)}) collective-permute-start(bf16[16,8192]{1,0:T(8,128)(2,1)S(1)} %get-tuple-element.40), channel_id=1, source_target_pairs={{0,1},{1,0},{2,3},{3,2},{4,5},{5,4},{6,7},{7,6},{8,9},{9,8},{10,11... | collective-permute-start | bytes 786440 | tf_op jit(solution)/shard_map/ppermute | solution.py:21
  46.8 4.2 %collective-permute-start.11 = (bf16[16,8192]{1,0:T(8,128)(2,1)S(1)}, bf16[16,8192]{1,0:T(8,128)(2,1)S(1)}, u32[]{:S(2)}, u32[]{:S(2)}) collective-permute-start(bf16[16,8192]{1,0:T(8,128)(2,1)S(1)} %get-tuple-element.42), channel_id=1, source_target_pairs={{0,1},{1,0},{2,3},{3,2},{4,5},{5,4},{6,7},{7,6},{8,9},{9,8},{10,11... | collective-permute-start | bytes 786440 | tf_op jit(solution)/shard_map/ppermute | solution.py:21
  47.1 4.9 %collective-permute-start.13 = (bf16[16,8192]{1,0:T(8,128)(2,1)S(1)}, bf16[16,8192]{1,0:T(8,128)(2,1)S(1)}, u32[]{:S(2)}, u32[]{:S(2)}) collective-permute-start(bf16[16,8192]{1,0:T(8,128)(2,1)S(1)} %get-tuple-element.44), channel_id=1, source_target_pairs={{0,1},{1,0},{2,3},{3,2},{4,5},{5,4},{6,7},{7,6},{8,9},{9,8},{10,11... | collective-permute-start | bytes 786440 | tf_op jit(solution)/shard_map/ppermute | solution.py:21
  49.0 8.5 %collective-permute-start.8 = (bf16[16,8192]{1,0:T(8,128)(2,1)S(1)}, bf16[16,8192]{1,0:T(8,128)(2,1)S(1)}, u32[]{:S(2)}, u32[]{:S(2)}) collective-permute-start(bf16[16,8192]{1,0:T(8,128)(2,1)S(1)} %add_convert_fusion.15), channel_id=1, source_target_pairs={{0,6},{1,7},{2,4},{3,5},{4,2},{5,3},{6,0},{7,1},{8,14},{9,15},{10,... | collective-permute-start | bytes 786440 | tf_op jit(solution)/shard_map/ppermute | solution.py:21
  50.4 13.5 %collective-permute-start.10 = (bf16[16,8192]{1,0:T(8,128)(2,1)S(1)}, bf16[16,8192]{1,0:T(8,128)(2,1)S(1)}, u32[]{:S(2)}, u32[]{:S(2)}) collective-permute-start(bf16[16,8192]{1,0:T(8,128)(2,1)S(1)} %add_convert_fusion.14), channel_id=1, source_target_pairs={{0,4},{1,5},{2,6},{3,7},{4,0},{5,1},{6,2},{7,3},{8,12},{9,13},{10,... | collective-permute-start | bytes 786440 | tf_op jit(solution)/shard_map/ppermute | solution.py:21
  51.0 12.8 %collective-permute-start.12 = (bf16[16,8192]{1,0:T(8,128)(2,1)S(1)}, bf16[16,8192]{1,0:T(8,128)(2,1)S(1)}, u32[]{:S(2)}, u32[]{:S(2)}) collective-permute-start(bf16[16,8192]{1,0:T(8,128)(2,1)S(1)} %add_convert_fusion.13), channel_id=1, source_target_pairs={{0,2},{1,3},{2,0},{3,1},{4,6},{5,7},{6,4},{7,5},{8,10},{9,11},{10,... | collective-permute-start | bytes 786440 | tf_op jit(solution)/shard_map/ppermute | solution.py:21
  64.0 0.7 collective-permute-start.14
  65.1 7.3 %collective-permute-start.16 = (bf16[16,8192]{1,0:T(8,128)(2,1)S(1)}, bf16[16,8192]{1,0:T(8,128)(2,1)S(1)}, u32[]{:S(2)}, u32[]{:S(2)}) collective-permute-start(bf16[16,8192]{1,0:T(8,128)(2,1)S(1)} %fusion.2.refs_0_), channel_id=1, source_target_pairs={{0,2},{1,3},{2,0},{3,1},{4,6},{5,7},{6,4},{7,5},{8,10},{9,11},{10,... | collective-permute-start | bytes 786440 | tf_op jit(solution)/shard_map/ppermute | solution.py:21
  65.7 9.2 %collective-permute-start.18 = (bf16[16,8192]{1,0:T(8,128)(2,1)S(1)}, bf16[16,8192]{1,0:T(8,128)(2,1)S(1)}, u32[]{:S(2)}, u32[]{:S(2)}) collective-permute-start(bf16[16,8192]{1,0:T(8,128)(2,1)S(1)} %fusion.2.refs_0_), channel_id=1, source_target_pairs={{0,4},{1,5},{2,6},{3,7},{4,0},{5,1},{6,2},{7,3},{8,12},{9,13},{10,... | collective-permute-start | bytes 786440 | tf_op jit(solution)/shard_map/ppermute | solution.py:21
  66.7 13.4 %collective-permute-start.20 = (bf16[16,8192]{1,0:T(8,128)(2,1)S(1)}, bf16[16,8192]{1,0:T(8,128)(2,1)S(1)}, u32[]{:S(2)}, u32[]{:S(2)}) collective-permute-start(bf16[16,8192]{1,0:T(8,128)(2,1)S(1)} %fusion.2.refs_0_), channel_id=1, source_target_pairs={{0,6},{1,7},{2,4},{3,5},{4,2},{5,3},{6,0},{7,1},{8,14},{9,15},{10,... | collective-permute-start | bytes 786440 | tf_op jit(solution)/shard_map/ppermute | solution.py:21
  67.8 12.4 %collective-permute-start.15 = (bf16[16,8192]{1,0:T(8,128)(2,1)S(1)}, bf16[16,8192]{1,0:T(8,128)(2,1)S(1)}, u32[]{:S(2)}, u32[]{:S(2)}) collective-permute-start(bf16[16,8192]{1,0:T(8,128)(2,1)S(1)} %fusion.2.refs_0_), channel_id=1, source_target_pairs={{0,1},{1,0},{2,3},{3,2},{4,5},{5,4},{6,7},{7,6},{8,9},{9,8},{10,11... | collective-permute-start | bytes 786440 | tf_op jit(solution)/shard_map/ppermute | solution.py:21
  72.4 7.7 %collective-permute-start.17 = (bf16[16,8192]{1,0:T(8,128)(2,1)S(1)}, bf16[16,8192]{1,0:T(8,128)(2,1)S(1)}, u32[]{:S(2)}, u32[]{:S(2)}) collective-permute-start(bf16[16,8192]{1,0:T(8,128)(2,1)S(1)} %collective-permute-done.16.refs_2_), channel_id=1, source_target_pairs={{0,1},{1,0},{2,3},{3,2},{4,5},{5,4},{6,7},{7,6},{8,9},{9,8},{10,11... | collective-permute-start | bytes 786440 | tf_op jit(solution)/shard_map/ppermute | solution.py:21
  74.9 6.3 %collective-permute-start.19 = (bf16[16,8192]{1,0:T(8,128)(2,1)S(1)}, bf16[16,8192]{1,0:T(8,128)(2,1)S(1)}, u32[]{:S(2)}, u32[]{:S(2)}) collective-permute-start(bf16[16,8192]{1,0:T(8,128)(2,1)S(1)} %collective-permute-done.18.refs_4_), channel_id=1, source_target_pairs={{0,1},{1,0},{2,3},{3,2},{4,5},{5,4},{6,7},{7,6},{8,9},{9,8},{10,11... | collective-permute-start | bytes 786440 | tf_op jit(solution)/shard_map/ppermute | solution.py:21
  80.1 1.5 collective-permute-start.21
  108.0 1.8 collective-permute-start.22
  108.4 3.8 %collective-permute-start.24 = (bf16[16,8192]{1,0:T(8,128)(2,1)S(1)}, bf16[16,8192]{1,0:T(8,128)(2,1)S(1)}, u32[]{:S(2)}, u32[]{:S(2)}) collective-permute-start(bf16[16,8192]{1,0:T(8,128)(2,1)S(1)} %get-tuple-element.48), channel_id=1, source_target_pairs={{0,1},{1,0},{2,3},{3,2},{4,5},{5,4},{6,7},{7,6},{8,9},{9,8},{10,11... | collective-permute-start | bytes 786440 | tf_op jit(solution)/shard_map/ppermute | solution.py:21
  108.6 4.5 %collective-permute-start.26 = (bf16[16,8192]{1,0:T(8,128)(2,1)S(1)}, bf16[16,8192]{1,0:T(8,128)(2,1)S(1)}, u32[]{:S(2)}, u32[]{:S(2)}) collective-permute-start(bf16[16,8192]{1,0:T(8,128)(2,1)S(1)} %get-tuple-element.50), channel_id=1, source_target_pairs={{0,1},{1,0},{2,3},{3,2},{4,5},{5,4},{6,7},{7,6},{8,9},{9,8},{10,11... | collective-permute-start | bytes 786440 | tf_op jit(solution)/shard_map/ppermute | solution.py:21
  109.0 4.9 %collective-permute-start.28 = (bf16[16,8192]{1,0:T(8,128)(2,1)S(1)}, bf16[16,8192]{1,0:T(8,128)(2,1)S(1)}, u32[]{:S(2)}, u32[]{:S(2)}) collective-permute-start(bf16[16,8192]{1,0:T(8,128)(2,1)S(1)} %get-tuple-element.52), channel_id=1, source_target_pairs={{0,1},{1,0},{2,3},{3,2},{4,5},{5,4},{6,7},{7,6},{8,9},{9,8},{10,11... | collective-permute-start | bytes 786440 | tf_op jit(solution)/shard_map/ppermute | solution.py:21
  110.8 8.5 %collective-permute-start.23 = (bf16[16,8192]{1,0:T(8,128)(2,1)S(1)}, bf16[16,8192]{1,0:T(8,128)(2,1)S(1)}, u32[]{:S(2)}, u32[]{:S(2)}) collective-permute-start(bf16[16,8192]{1,0:T(8,128)(2,1)S(1)} %add_convert_fusion.11), channel_id=1, source_target_pairs={{0,6},{1,7},{2,4},{3,5},{4,2},{5,3},{6,0},{7,1},{8,14},{9,15},{10,... | collective-permute-start | bytes 786440 | tf_op jit(solution)/shard_map/ppermute | solution.py:21
  112.3 13.3 %collective-permute-start.25 = (bf16[16,8192]{1,0:T(8,128)(2,1)S(1)}, bf16[16,8192]{1,0:T(8,128)(2,1)S(1)}, u32[]{:S(2)}, u32[]{:S(2)}) collective-permute-start(bf16[16,8192]{1,0:T(8,128)(2,1)S(1)} %add_convert_fusion.10), channel_id=1, source_target_pairs={{0,4},{1,5},{2,6},{3,7},{4,0},{5,1},{6,2},{7,3},{8,12},{9,13},{10,... | collective-permute-start | bytes 786440 | tf_op jit(solution)/shard_map/ppermute | solution.py:21
  113.2 12.5 %collective-permute-start.27 = (bf16[16,8192]{1,0:T(8,128)(2,1)S(1)}, bf16[16,8192]{1,0:T(8,128)(2,1)S(1)}, u32[]{:S(2)}, u32[]{:S(2)}) collective-permute-start(bf16[16,8192]{1,0:T(8,128)(2,1)S(1)} %add_convert_fusion.9), channel_id=1, source_target_pairs={{0,2},{1,3},{2,0},{3,1},{4,6},{5,7},{6,4},{7,5},{8,10},{9,11},{10,... | collective-permute-start | bytes 786440 | tf_op jit(solution)/shard_map/ppermute | solution.py:21
  125.9 0.9 collective-permute-start.29
  127.1 16.9 %copy-start.5 = (bf16[16,8192]{1,0:T(8,128)(2,1)}, bf16[16,8192]{1,0:T(8,128)(2,1)S(1)}, u32[]{:S(2)}) copy-start(bf16[16,8192]{1,0:T(8,128)(2,1)S(1)} %fusion.6.refs_0_) | copy-start | bytes 786436
  127.1 7.4 %collective-permute-start.31 = (bf16[16,8192]{1,0:T(8,128)(2,1)S(1)}, bf16[16,8192]{1,0:T(8,128)(2,1)S(1)}, u32[]{:S(2)}, u32[]{:S(2)}) collective-permute-start(bf16[16,8192]{1,0:T(8,128)(2,1)S(1)} %fusion.6.refs_0_), channel_id=1, source_target_pairs={{0,2},{1,3},{2,0},{3,1},{4,6},{5,7},{6,4},{7,5},{8,10},{9,11},{10,... | collective-permute-start | bytes 786440 | tf_op jit(solution)/shard_map/ppermute | solution.py:21
  128.1 8.8 %collective-permute-start.33 = (bf16[16,8192]{1,0:T(8,128)(2,1)S(1)}, bf16[16,8192]{1,0:T(8,128)(2,1)S(1)}, u32[]{:S(2)}, u32[]{:S(2)}) collective-permute-start(bf16[16,8192]{1,0:T(8,128)(2,1)S(1)} %fusion.6.refs_0_), channel_id=1, source_target_pairs={{0,4},{1,5},{2,6},{3,7},{4,0},{5,1},{6,2},{7,3},{8,12},{9,13},{10,... | collective-permute-start | bytes 786440 | tf_op jit(solution)/shard_map/ppermute | solution.py:21
  128.8 13.6 %collective-permute-start.35 = (bf16[16,8192]{1,0:T(8,128)(2,1)S(1)}, bf16[16,8192]{1,0:T(8,128)(2,1)S(1)}, u32[]{:S(2)}, u32[]{:S(2)}) collective-permute-start(bf16[16,8192]{1,0:T(8,128)(2,1)S(1)} %fusion.6.refs_0_), channel_id=1, source_target_pairs={{0,6},{1,7},{2,4},{3,5},{4,2},{5,3},{6,0},{7,1},{8,14},{9,15},{10,... | collective-permute-start | bytes 786440 | tf_op jit(solution)/shard_map/ppermute | solution.py:21
  129.8 12.7 %collective-permute-start.30 = (bf16[16,8192]{1,0:T(8,128)(2,1)S(1)}, bf16[16,8192]{1,0:T(8,128)(2,1)S(1)}, u32[]{:S(2)}, u32[]{:S(2)}) collective-permute-start(bf16[16,8192]{1,0:T(8,128)(2,1)S(1)} %fusion.6.refs_0_), channel_id=1, source_target_pairs={{0,1},{1,0},{2,3},{3,2},{4,5},{5,4},{6,7},{7,6},{8,9},{9,8},{10,11... | collective-permute-start | bytes 786440 | tf_op jit(solution)/shard_map/ppermute | solution.py:21
  134.5 7.9 %collective-permute-start.32 = (bf16[16,8192]{1,0:T(8,128)(2,1)S(1)}, bf16[16,8192]{1,0:T(8,128)(2,1)S(1)}, u32[]{:S(2)}, u32[]{:S(2)}) collective-permute-start(bf16[16,8192]{1,0:T(8,128)(2,1)S(1)} %collective-permute-done.31.refs_2_), channel_id=1, source_target_pairs={{0,1},{1,0},{2,3},{3,2},{4,5},{5,4},{6,7},{7,6},{8,9},{9,8},{10,11... | collective-permute-start | bytes 786440 | tf_op jit(solution)/shard_map/ppermute | solution.py:21
  136.8 6.7 %collective-permute-start.34 = (bf16[16,8192]{1,0:T(8,128)(2,1)S(1)}, bf16[16,8192]{1,0:T(8,128)(2,1)S(1)}, u32[]{:S(2)}, u32[]{:S(2)}) collective-permute-start(bf16[16,8192]{1,0:T(8,128)(2,1)S(1)} %collective-permute-done.33.refs_4_), channel_id=1, source_target_pairs={{0,1},{1,0},{2,3},{3,2},{4,5},{5,4},{6,7},{7,6},{8,9},{9,8},{10,11... | collective-permute-start | bytes 786440 | tf_op jit(solution)/shard_map/ppermute | solution.py:21
  142.4 1.5 collective-permute-start.36
  170.3 1.8 collective-permute-start.37
  170.8 3.7 %collective-permute-start.39 = (bf16[16,8192]{1,0:T(8,128)(2,1)S(1)}, bf16[16,8192]{1,0:T(8,128)(2,1)S(1)}, u32[]{:S(2)}, u32[]{:S(2)}) collective-permute-start(bf16[16,8192]{1,0:T(8,128)(2,1)S(1)} %get-tuple-element.56), channel_id=1, source_target_pairs={{0,1},{1,0},{2,3},{3,2},{4,5},{5,4},{6,7},{7,6},{8,9},{9,8},{10,11... | collective-permute-start | bytes 786440 | tf_op jit(solution)/shard_map/ppermute | solution.py:21
  170.9 4.2 %collective-permute-start.41 = (bf16[16,8192]{1,0:T(8,128)(2,1)S(1)}, bf16[16,8192]{1,0:T(8,128)(2,1)S(1)}, u32[]{:S(2)}, u32[]{:S(2)}) collective-permute-start(bf16[16,8192]{1,0:T(8,128)(2,1)S(1)} %get-tuple-element.58), channel_id=1, source_target_pairs={{0,1},{1,0},{2,3},{3,2},{4,5},{5,4},{6,7},{7,6},{8,9},{9,8},{10,11... | collective-permute-start | bytes 786440 | tf_op jit(solution)/shard_map/ppermute | solution.py:21
  171.3 4.9 %collective-permute-start.43 = (bf16[16,8192]{1,0:T(8,128)(2,1)S(1)}, bf16[16,8192]{1,0:T(8,128)(2,1)S(1)}, u32[]{:S(2)}, u32[]{:S(2)}) collective-permute-start(bf16[16,8192]{1,0:T(8,128)(2,1)S(1)} %get-tuple-element.60), channel_id=1, source_target_pairs={{0,1},{1,0},{2,3},{3,2},{4,5},{5,4},{6,7},{7,6},{8,9},{9,8},{10,11... | collective-permute-start | bytes 786440 | tf_op jit(solution)/shard_map/ppermute | solution.py:21
  173.2 8.5 %collective-permute-start.38 = (bf16[16,8192]{1,0:T(8,128)(2,1)S(1)}, bf16[16,8192]{1,0:T(8,128)(2,1)S(1)}, u32[]{:S(2)}, u32[]{:S(2)}) collective-permute-start(bf16[16,8192]{1,0:T(8,128)(2,1)S(1)} %add_convert_fusion.7), channel_id=1, source_target_pairs={{0,6},{1,7},{2,4},{3,5},{4,2},{5,3},{6,0},{7,1},{8,14},{9,15},{10,... | collective-permute-start | bytes 786440 | tf_op jit(solution)/shard_map/ppermute | solution.py:21
  174.5 13.5 %collective-permute-start.40 = (bf16[16,8192]{1,0:T(8,128)(2,1)S(1)}, bf16[16,8192]{1,0:T(8,128)(2,1)S(1)}, u32[]{:S(2)}, u32[]{:S(2)}) collective-permute-start(bf16[16,8192]{1,0:T(8,128)(2,1)S(1)} %add_convert_fusion.6), channel_id=1, source_target_pairs={{0,4},{1,5},{2,6},{3,7},{4,0},{5,1},{6,2},{7,3},{8,12},{9,13},{10,... | collective-permute-start | bytes 786440 | tf_op jit(solution)/shard_map/ppermute | solution.py:21
  175.2 12.8 %collective-permute-start.42 = (bf16[16,8192]{1,0:T(8,128)(2,1)S(1)}, bf16[16,8192]{1,0:T(8,128)(2,1)S(1)}, u32[]{:S(2)}, u32[]{:S(2)}) collective-permute-start(bf16[16,8192]{1,0:T(8,128)(2,1)S(1)} %add_convert_fusion.5), channel_id=1, source_target_pairs={{0,2},{1,3},{2,0},{3,1},{4,6},{5,7},{6,4},{7,5},{8,10},{9,11},{10,... | collective-permute-start | bytes 786440 | tf_op jit(solution)/shard_map/ppermute | solution.py:21
  188.2 23.0 %collective-permute-start.44 = (bf16[16,8192]{1,0:T(8,128)(2,1)S(1)}, bf16[16,8192]{1,0:T(8,128)(2,1)S(1)}, u32[]{:S(2)}, u32[]{:S(2)}) collective-permute-start(bf16[16,8192]{1,0:T(8,128)(2,1)S(1)} %fusion.7), channel_id=1, source_target_pairs={{16,24},{17,25},{18,26},{19,27},{20,28},{21,29},{22,30},{23,31}} | collective-permute-start | bytes 786440 | tf_op jit(solution)/shard_map/ppermute | solution.py:25
  211.5 16.7 %copy-start.3 = (bf16[16,8192]{1,0:T(8,128)(2,1)}, bf16[16,8192]{1,0:T(8,128)(2,1)S(1)}, u32[]{:S(2)}) copy-start(bf16[16,8192]{1,0:T(8,128)(2,1)S(1)} %fusion.10.refs_0_) | copy-start | bytes 786436
  211.5 6.8 %collective-permute-start.46 = (bf16[16,8192]{1,0:T(8,128)(2,1)S(1)}, bf16[16,8192]{1,0:T(8,128)(2,1)S(1)}, u32[]{:S(2)}, u32[]{:S(2)}) collective-permute-start(bf16[16,8192]{1,0:T(8,128)(2,1)S(1)} %fusion.10.refs_0_), channel_id=1, source_target_pairs={{0,2},{1,3},{2,0},{3,1},{4,6},{5,7},{6,4},{7,5},{8,10},{9,11},{10,... | collective-permute-start | bytes 786440 | tf_op jit(solution)/shard_map/ppermute | solution.py:21
  212.3 9.6 %collective-permute-start.48 = (bf16[16,8192]{1,0:T(8,128)(2,1)S(1)}, bf16[16,8192]{1,0:T(8,128)(2,1)S(1)}, u32[]{:S(2)}, u32[]{:S(2)}) collective-permute-start(bf16[16,8192]{1,0:T(8,128)(2,1)S(1)} %fusion.10.refs_0_), channel_id=1, source_target_pairs={{0,4},{1,5},{2,6},{3,7},{4,0},{5,1},{6,2},{7,3},{8,12},{9,13},{10,... | collective-permute-start | bytes 786440 | tf_op jit(solution)/shard_map/ppermute | solution.py:21
  213.2 13.4 %collective-permute-start.50 = (bf16[16,8192]{1,0:T(8,128)(2,1)S(1)}, bf16[16,8192]{1,0:T(8,128)(2,1)S(1)}, u32[]{:S(2)}, u32[]{:S(2)}) collective-permute-start(bf16[16,8192]{1,0:T(8,128)(2,1)S(1)} %fusion.10.refs_0_), channel_id=1, source_target_pairs={{0,6},{1,7},{2,4},{3,5},{4,2},{5,3},{6,0},{7,1},{8,14},{9,15},{10,... | collective-permute-start | bytes 786440 | tf_op jit(solution)/shard_map/ppermute | solution.py:21
  214.2 12.5 %collective-permute-start.45 = (bf16[16,8192]{1,0:T(8,128)(2,1)S(1)}, bf16[16,8192]{1,0:T(8,128)(2,1)S(1)}, u32[]{:S(2)}, u32[]{:S(2)}) collective-permute-start(bf16[16,8192]{1,0:T(8,128)(2,1)S(1)} %fusion.10.refs_0_), channel_id=1, source_target_pairs={{0,1},{1,0},{2,3},{3,2},{4,5},{5,4},{6,7},{7,6},{8,9},{9,8},{10,11... | collective-permute-start | bytes 786440 | tf_op jit(solution)/shard_map/ppermute | solution.py:21
  218.4 8.3 %collective-permute-start.47 = (bf16[16,8192]{1,0:T(8,128)(2,1)S(1)}, bf16[16,8192]{1,0:T(8,128)(2,1)S(1)}, u32[]{:S(2)}, u32[]{:S(2)}) collective-permute-start(bf16[16,8192]{1,0:T(8,128)(2,1)S(1)} %collective-permute-done.46.refs_2_), channel_id=1, source_target_pairs={{0,1},{1,0},{2,3},{3,2},{4,5},{5,4},{6,7},{7,6},{8,9},{9,8},{10,11... | collective-permute-start | bytes 786440 | tf_op jit(solution)/shard_map/ppermute | solution.py:21
  221.8 5.9 %collective-permute-start.49 = (bf16[16,8192]{1,0:T(8,128)(2,1)S(1)}, bf16[16,8192]{1,0:T(8,128)(2,1)S(1)}, u32[]{:S(2)}, u32[]{:S(2)}) collective-permute-start(bf16[16,8192]{1,0:T(8,128)(2,1)S(1)} %collective-permute-done.48.refs_4_), channel_id=1, source_target_pairs={{0,1},{1,0},{2,3},{3,2},{4,5},{5,4},{6,7},{7,6},{8,9},{9,8},{10,11... | collective-permute-start | bytes 786440 | tf_op jit(solution)/shard_map/ppermute | solution.py:21
  226.6 1.5 collective-permute-start.51
  254.5 1.8 collective-permute-start.52
  255.0 3.5 %collective-permute-start.54 = (bf16[16,8192]{1,0:T(8,128)(2,1)S(1)}, bf16[16,8192]{1,0:T(8,128)(2,1)S(1)}, u32[]{:S(2)}, u32[]{:S(2)}) collective-permute-start(bf16[16,8192]{1,0:T(8,128)(2,1)S(1)} %get-tuple-element.64), channel_id=1, source_target_pairs={{0,1},{1,0},{2,3},{3,2},{4,5},{5,4},{6,7},{7,6},{8,9},{9,8},{10,11... | collective-permute-start | bytes 786440 | tf_op jit(solution)/shard_map/ppermute | solution.py:21
  255.1 4.4 %collective-permute-start.56 = (bf16[16,8192]{1,0:T(8,128)(2,1)S(1)}, bf16[16,8192]{1,0:T(8,128)(2,1)S(1)}, u32[]{:S(2)}, u32[]{:S(2)}) collective-permute-start(bf16[16,8192]{1,0:T(8,128)(2,1)S(1)} %get-tuple-element.66), channel_id=1, source_target_pairs={{0,1},{1,0},{2,3},{3,2},{4,5},{5,4},{6,7},{7,6},{8,9},{9,8},{10,11... | collective-permute-start | bytes 786440 | tf_op jit(solution)/shard_map/ppermute | solution.py:21
  255.5 4.9 %collective-permute-start.58 = (bf16[16,8192]{1,0:T(8,128)(2,1)S(1)}, bf16[16,8192]{1,0:T(8,128)(2,1)S(1)}, u32[]{:S(2)}, u32[]{:S(2)}) collective-permute-start(bf16[16,8192]{1,0:T(8,128)(2,1)S(1)} %get-tuple-element.68), channel_id=1, source_target_pairs={{0,1},{1,0},{2,3},{3,2},{4,5},{5,4},{6,7},{7,6},{8,9},{9,8},{10,11... | collective-permute-start | bytes 786440 | tf_op jit(solution)/shard_map/ppermute | solution.py:21
  257.4 8.5 %collective-permute-start.53 = (bf16[16,8192]{1,0:T(8,128)(2,1)S(1)}, bf16[16,8192]{1,0:T(8,128)(2,1)S(1)}, u32[]{:S(2)}, u32[]{:S(2)}) collective-permute-start(bf16[16,8192]{1,0:T(8,128)(2,1)S(1)} %add_convert_fusion.3), channel_id=1, source_target_pairs={{0,6},{1,7},{2,4},{3,5},{4,2},{5,3},{6,0},{7,1},{8,14},{9,15},{10,... | collective-permute-start | bytes 786440 | tf_op jit(solution)/shard_map/ppermute | solution.py:21
  258.5 13.7 %collective-permute-start.55 = (bf16[16,8192]{1,0:T(8,128)(2,1)S(1)}, bf16[16,8192]{1,0:T(8,128)(2,1)S(1)}, u32[]{:S(2)}, u32[]{:S(2)}) collective-permute-start(bf16[16,8192]{1,0:T(8,128)(2,1)S(1)} %add_convert_fusion.2), channel_id=1, source_target_pairs={{0,4},{1,5},{2,6},{3,7},{4,0},{5,1},{6,2},{7,3},{8,12},{9,13},{10,... | collective-permute-start | bytes 786440 | tf_op jit(solution)/shard_map/ppermute | solution.py:21
  259.6 12.6 %collective-permute-start.57 = (bf16[16,8192]{1,0:T(8,128)(2,1)S(1)}, bf16[16,8192]{1,0:T(8,128)(2,1)S(1)}, u32[]{:S(2)}, u32[]{:S(2)}) collective-permute-start(bf16[16,8192]{1,0:T(8,128)(2,1)S(1)} %add_convert_fusion.1), channel_id=1, source_target_pairs={{0,2},{1,3},{2,0},{3,1},{4,6},{5,7},{6,4},{7,5},{8,10},{9,11},{10,... | collective-permute-start | bytes 786440 | tf_op jit(solution)/shard_map/ppermute | solution.py:21
  (30 other events, 105.7 us)
